TPU v7x, 512 devices: a whole 4x8x8 slice. The times are simulated.
512 devices in a mesh: lat: 16 (over x, z_hi, core), lon: 32 (over y, z_lo).
Axes of the slice: x: 4, y: 8, z: 8 (z_hi: 2, z_lo: 4; z = z_hi * 4 + z_lo), core: 2. Of those that a mesh axis runs over, the one named last changes fastest.
Arguments:
- inputs_below: bfloat16 [64, 128, 4096], P(None, 'lat', 'lon'), may hold values from -6 to 6
- hidden_prev: bfloat16 [64, 128, 4096], P(None, 'lat', 'lon'), may hold values from -0.8984375 to 0.8984375
- cell_prev: float32 [64, 128, 4096], P(None, 'lat', 'lon'), may hold values from -5 to 5
- kernel_weights: bfloat16 [9, 256, 128], replicated, may hold values from -0.1875 to 0.1875
- gate_bias: float32 [256], replicated, may hold values from -4 to 4
- readout: float32 [64], replicated, may hold values from -0.75 to 0.75
- target_field: float32 [128, 4096], P('lat', 'lon'), may hold values from -6 to 6
- land_mask: int32 [128, 4096], P('lat', 'lon'), may hold values 0 or 1
- fire_mask: int32 [128, 4096], P('lat', 'lon'), may hold values 0 or 1
- hidden_grad: bfloat16 [64, 128, 4096], P(None, 'lat', 'lon'), may hold values from -10 to 10
Outputs:
- hidden_next: bfloat16 [64, 128, 4096], P(None, 'lat', 'lon')
- cell_next: float32 [64, 128, 4096], P(None, 'lat', 'lon')
- grad_inputs: bfloat16 [64, 128, 4096], P(None, 'lat', 'lon')
- grad_hidden: bfloat16 [64, 128, 4096], P(None, 'lat', 'lon')
- grad_cell: float32 [64, 128, 4096], P(None, 'lat', 'lon')
- grad_kernel: float32 [9, 256, 128], replicated
- grad_bias: float32 [256], replicated
Inputs may be any that keep to these rules, and one draw needn't show every extreme that they name: `land_mask`: 1 marks land cells, 0 sea cells. `fire_mask`: 1 marks cells where fire danger is observed.
All inputs are finite; a program needn't handle non-finite values. No bound on the sum of `land_mask` or of `fire_mask` on one device may be relied on, other than what follows from the above.
Results may differ from a plain program's by a relative error of at most 0.0049.
Values may be sent and summed in bfloat16 or wider, within the bound.
A program may use at most 64 MiB of HBM per device.

v0:
```python
import math
import jax
import jax.numpy as jnp
from jax import lax
from jax.sharding import PartitionSpec as P


def with_halo(cells, sides, width, closed):
    for axis, dim in sides:
        count = lax.axis_size(axis)
        ends = count if closed else count - 1
        head = lax.slice_in_dim(cells, 0, width, axis=dim)
        tail = lax.slice_in_dim(cells, cells.shape[dim] - width, cells.shape[dim], axis=dim)
        cells = jnp.concatenate(
            [
                lax.ppermute(tail, axis, [(i, (i + 1) % count) for i in range(ends)]),
                cells,
                lax.ppermute(head, axis, [((i + 1) % count, i) for i in range(ends)]),
            ],
            axis=dim,
        )
    return cells


def shifted(value, axis, steps):
    count = lax.axis_size(axis)
    pairs = [(source, (source + steps) % count) for source in range(count)]
    return lax.ppermute(value, axis, pairs)


def extend(field):
    banded = with_halo(field, (("lat", 1),), 1, False)
    edge_rows = jnp.concatenate([field[:, :1], field[:, -1:]], axis=1)
    across = shifted(edge_rows, "lon", lax.axis_size("lon") // 2)
    band_index = lax.axis_index("lat")
    northern = band_index == 0
    southern = band_index == lax.axis_size("lat") - 1
    top_row = jnp.where(northern, across[:, :1], banded[:, :1])
    bottom_row = jnp.where(southern, across[:, 1:], banded[:, -1:])
    joined = jnp.concatenate([top_row, banded[:, 1:-1], bottom_row], axis=1)
    return with_halo(joined, (("lon", 2),), 1, True)


def windows(padded, row_count, col_count, flipped):
    result = []
    for position in range(9):
        lat_start = position // 3
        lon_start = position % 3
        if flipped:
            lat_start = 2 - lat_start
            lon_start = 2 - lon_start
        result.append(
            padded[:, lat_start : lat_start + row_count, lon_start : lon_start + col_count]
        )
    return result


def body(
    inputs_below,
    hidden_prev,
    cell_prev,
    kernel_weights,
    gate_bias,
    readout,
    target_field,
    land_mask,
    fire_mask,
    hidden_grad,
):
    hidden_width = hidden_prev.shape[0]
    input_width = inputs_below.shape[0]
    gate_count = kernel_weights.shape[1]
    channels = kernel_weights.shape[2]
    row_count = cell_prev.shape[1]
    col_count = cell_prev.shape[2]
    stacked = jnp.concatenate([inputs_below, hidden_prev], axis=0)
    padded = extend(stacked)
    forward_windows = windows(padded, row_count, col_count, False)
    preact = jnp.zeros((gate_count, row_count, col_count), jnp.float32)
    for position in range(9):
        preact = preact + jnp.einsum(
            "gc,crw->grw",
            kernel_weights[position],
            forward_windows[position],
            preferred_element_type=jnp.float32,
        )
    preact = preact + gate_bias[:, None, None]
    input_gate = jax.nn.sigmoid(preact[0:hidden_width])
    forget_gate = jax.nn.sigmoid(preact[hidden_width : 2 * hidden_width])
    output_gate = jax.nn.sigmoid(preact[2 * hidden_width : 3 * hidden_width])
    candidate = jnp.tanh(preact[3 * hidden_width : 4 * hidden_width])
    land_float = land_mask.astype(jnp.float32)[None]
    fire_float = fire_mask.astype(jnp.float32)
    cell_next = land_float * (forget_gate * cell_prev + input_gate * candidate)
    squashed = jnp.tanh(cell_next)
    hidden_next = (output_gate * squashed).astype(jnp.bfloat16)
    predicted = jnp.sum(readout[:, None, None] * hidden_next.astype(jnp.float32), axis=0)
    total_grad = (
        hidden_grad.astype(jnp.float32)
        + 2.0 * (fire_float * (predicted - target_field))[None] * readout[:, None, None]
    )
    cell_grad = land_float * total_grad * output_gate * (1.0 - squashed * squashed)
    grad_cell = cell_grad * forget_gate
    pre_grad = jnp.concatenate(
        [
            cell_grad * candidate * input_gate * (1.0 - input_gate),
            cell_grad * cell_prev * forget_gate * (1.0 - forget_gate),
            total_grad * squashed * output_gate * (1.0 - output_gate),
            cell_grad * input_gate * (1.0 - candidate * candidate),
        ],
        axis=0,
    )
    pre_low = pre_grad.astype(jnp.bfloat16)
    local_bias = jnp.sum(pre_grad, axis=(1, 2))
    local_kernel = jnp.stack(
        [
            jnp.einsum(
                "grw,crw->gc",
                pre_low,
                forward_windows[position],
                preferred_element_type=jnp.float32,
            )
            for position in range(9)
        ],
        axis=0,
    )
    grad_padded = extend(pre_low)
    band_index = lax.axis_index("lat")
    northern = band_index == 0
    southern = band_index == lax.axis_size("lat") - 1
    row_index = lax.broadcasted_iota(jnp.int32, (1, row_count + 2, 1), 1)
    pole_rows = northern & (row_index == 0) | southern & (row_index == row_count + 1)
    main_padded = jnp.where(pole_rows, jnp.zeros_like(grad_padded), grad_padded)
    back_windows = windows(main_padded, row_count, col_count, True)
    field_grad = jnp.zeros((channels, row_count, col_count), jnp.float32)
    for position in range(9):
        field_grad = field_grad + jnp.einsum(
            "gc,grw->crw",
            kernel_weights[position],
            back_windows[position],
            preferred_element_type=jnp.float32,
        )
    north_term = jnp.zeros((channels, col_count), jnp.float32)
    south_term = jnp.zeros((channels, col_count), jnp.float32)
    for position in range(3):
        lon_start = 2 - position
        north_term = north_term + jnp.einsum(
            "gc,gw->cw",
            kernel_weights[position],
            grad_padded[:, 0, lon_start : lon_start + col_count],
            preferred_element_type=jnp.float32,
        )
        south_term = south_term + jnp.einsum(
            "gc,gw->cw",
            kernel_weights[6 + position],
            grad_padded[:, row_count + 1, lon_start : lon_start + col_count],
            preferred_element_type=jnp.float32,
        )
    field_grad = field_grad.at[:, 0].add(jnp.where(northern, north_term, 0.0))
    field_grad = field_grad.at[:, row_count - 1].add(jnp.where(southern, south_term, 0.0))
    grad_inputs = field_grad[:input_width].astype(jnp.bfloat16)
    grad_hidden = field_grad[input_width:].astype(jnp.bfloat16)
    scaling = 1.0 / math.sqrt(row_count * lax.axis_size("lat") * col_count * lax.axis_size("lon"))
    summed_kernel, summed_bias = lax.psum((local_kernel, local_bias), ("lat", "lon"))
    grad_kernel = summed_kernel * scaling
    grad_bias = summed_bias * scaling
    return (hidden_next, cell_next, grad_inputs, grad_hidden, grad_cell, grad_kernel, grad_bias)


def solution(mesh):
    return jax.shard_map(
        body,
        mesh=mesh,
        in_specs=(
            P(None, "lat", "lon"),
            P(None, "lat", "lon"),
            P(None, "lat", "lon"),
            P(),
            P(),
            P(),
            P("lat", "lon"),
            P("lat", "lon"),
            P("lat", "lon"),
            P(None, "lat", "lon"),
        ),
        out_specs=(
            P(None, "lat", "lon"),
            P(None, "lat", "lon"),
            P(None, "lat", "lon"),
            P(None, "lat", "lon"),
            P(None, "lat", "lon"),
            P(),
            P(),
        ),
        check_vma=False,
    )
```

profile of v0, /device:TPU:1, one launch (start us, length us, event | category | flops | bytes accessed | tf_op | source)
XLA Modules:
  0.0 486.5 jit_solution(17038042296153973256)
XLA Ops:
  7.2 1.1 copy.215
  8.4 1.1 copy.216
  9.6 12.0 %collective-permute-start.1 = (bf16[128,1,128]{0,2,1:T(8,128)(2,1)S(1)}, bf16[128,1,128]{0,2,1:T(8,128)(2,1)S(1)}, u32[]{:S(2)}, u32[]{:S(2)}) collective-permute-start(bf16[128,1,128]{0,2,1:T(8,128)(2,1)S(1)} %get-tuple-element.98), channel_id=1, source_target_pairs={{0,32},{32,64},{64,96},{96,128},{128,160},{160,192},{192,224},{224... | collective-permute-start | bytes 98312 | tf_op jit(solution)/shard_map/ppermute | solution.py:16
  21.6 1.9 collective-permute-start.2
  23.6 7.5 %collective-permute-start = (bf16[128,2,128]{0,2,1:T(8,128)(2,1)S(1)}, bf16[128,2,128]{0,2,1:T(8,128)(2,1)S(1)}, u32[]{:S(2)}, u32[]{:S(2)}) collective-permute-start(bf16[128,2,128]{0,2,1:T(8,128)(2,1)S(1)} %pad_maximum_fusion.13), channel_id=1, source_target_pairs={{0,16},{1,17},{2,18},{3,19},{4,20},{5,21},{6,22},{7,23},{8,24},{9,... | collective-permute-start | bytes 196616 | tf_op jit(solution)/shard_map/ppermute | solution.py:28
  31.0 0.3 fusion.105
  31.4 1.3 copy.221
  32.8 0.3 fusion.30
  33.2 3.1 collective-permute-start.3
  36.3 7.1 %collective-permute-start.4 = (bf16[128,10,1]{0,2,1:T(2,128)(2,1)S(1)}, bf16[128,10,1]{0,2,1:T(2,128)(2,1)S(1)}, u32[]{:S(2)}, u32[]{:S(2)}) collective-permute-start(bf16[128,10,1]{0,2,1:T(2,128)(2,1)S(1)} %get-tuple-element.95), channel_id=1, source_target_pairs={{1,0},{2,1},{3,2},{4,3},{5,4},{6,5},{7,6},{8,7},{9,8},{10,9},{11,1... | collective-permute-start | bytes 7688 | tf_op jit(solution)/shard_map/ppermute | solution.py:18
  43.4 0.4 fusion.36
  43.8 1.3 copy.218
  45.1 1.3 copy.224
  46.4 0.3 maximum_maximum_fusion
  46.8 1.3 fusion.77
  48.1 0.3 fusion.71
  48.4 1.3 fusion.74
  49.6 1.4 fusion.68
  51.0 1.3 fusion.65
  52.3 0.3 fusion.62
  52.6 2.5 copy.217
  55.1 2.6 copy.219
  57.7 1.3 copy.220
  59.0 2.6 copy.222
  61.6 1.4 copy.223
  63.1 1.3 copy.225
  64.4 3.9 add_bitcast_fusion
  68.3 1.0 multiply_reduce_fusion
  69.3 0.9 fusion.157
  70.6 0.9 copy-done.7
  71.5 0.9 fusion.9
  72.6 9.0 %collective-permute-start.6 = (bf16[256,1,128]{2,1,0:T(2,128)(2,1)S(1)}, bf16[256,1,128]{2,1,0:T(2,128)(2,1)S(1)}, u32[]{:S(2)}, u32[]{:S(2)}) collective-permute-start(bf16[256,1,128]{2,1,0:T(2,128)(2,1)S(1)} %get-tuple-element.96), channel_id=1, source_target_pairs={{0,32},{32,64},{64,96},{96,128},{128,160},{160,192},{192,224},{224... | collective-permute-start | bytes 196616 | tf_op jit(solution)/shard_map/ppermute | solution.py:16
  81.6 0.3 pad_maximum_fusion.12
  81.9 1.9 collective-permute-start.7
  83.8 1.0 fusion.8
  84.8 1.0 fusion.7
  85.8 0.9 fusion.6
  86.7 1.0 fusion.5
  87.8 1.0 fusion.4
  88.8 0.9 fusion.3
  89.7 1.0 fusion.2
  90.8 7.1 %collective-permute-start.5 = (bf16[256,2,128]{2,1,0:T(2,128)(2,1)S(1)}, bf16[256,2,128]{2,1,0:T(2,128)(2,1)S(1)}, u32[]{:S(2)}, u32[]{:S(2)}) collective-permute-start(bf16[256,2,128]{2,1,0:T(2,128)(2,1)S(1)} %pad_maximum_fusion.12), channel_id=1, source_target_pairs={{0,16},{1,17},{2,18},{3,19},{4,20},{5,21},{6,22},{7,23},{8,24},{9,... | collective-permute-start | bytes 393224 | tf_op jit(solution)/shard_map/ppermute | solution.py:28
  97.9 1.0 fusion.1
  98.9 1.0 fusion.18
  99.9 98.2 %psum.15 = f32[256]{0:T(256)S(1)} all-reduce(f32[256]{0:T(256)S(1)} %fusion.18), channel_id=1, replica_groups=mesh['lat'=16,'lon'=32] {'lat','lon'}, use_global_device_ids=true, to_apply=%region_3.4 | all-reduce | flops 256 | bytes 2048 | tf_op jit(solution)/shard_map/psum | solution.py:164
  198.1 0.4 broadcast_select_fusion.1
  198.5 0.6 pad_maximum_fusion.1
  199.2 0.5 fusion.159
  199.6 0.9 copy.226
  200.5 3.2 collective-permute-start.8
  203.8 0.9 copy.227
  204.7 5.9 %collective-permute-start.9 = (bf16[256,10,1]{0,1,2:T(8,128)(2,1)S(1)}, bf16[256,10,1]{0,1,2:T(8,128)(2,1)S(1)}, u32[]{:S(2)}, u32[]{:S(2)}) collective-permute-start(bf16[256,10,1]{0,1,2:T(8,128)(2,1)S(1)} %copy.227), channel_id=1, source_target_pairs={{1,0},{2,1},{3,2},{4,3},{5,4},{6,5},{7,6},{8,7},{9,8},{10,9},{11,1... | collective-permute-start | bytes 15368 | tf_op jit(solution)/shard_map/ppermute | solution.py:18
  210.6 0.6 broadcast_multiply_fusion.1
  211.2 1.0 copy.228
  212.3 1.0 copy.229
  213.3 1.5 pad_maximum_fusion.4
  215.5 2.7 maximum_select_fusion
  218.2 1.4 fusion.158
  221.0 0.3 convolution_add_fusion.3
  221.3 0.3 convolution_add_fusion.2
  222.9 0.7 copy.268
  223.6 0.7 copy.269
  224.4 252.9 %all-reduce.2.cloned.1.call-done = f32[9,256,128]{2,1,0:T(8,128)} async-done(((f32[9,256,128]{2,1,0:T(8,128)}), f32[9,256,128]{2,1,0:T(8,128)}) %all-reduce.2.cloned.1.call-update) | async-done | bytes 1179664 | tf_op jit(solution)/shard_map/psum | solution.py:164
  477.3 2.4 broadcast_multiply_fusion
  (68 shorter events, 4.1 us)
Async XLA Ops:
  7.2 23.9 %copy-start.1 = (bf16[9,256,128]{2,1,0:T(8,128)(2,1)S(1)}, bf16[9,256,128]{2,1,0:T(8,128)(2,1)}, u32[]{:S(2)}) copy-start(bf16[9,256,128]{2,1,0:T(8,128)(2,1)} %param.17) | copy-start | bytes 1769476
  7.2 470.1 %all-reduce.2.cloned.1.call-start = ((), (), s32[]{:S(2)}) async-start(), calls=%async_computation | async-start | bytes 2359296 | tf_op jit(solution)/shard_map/psum | solution.py:164
  9.6 23.2 %collective-permute-start.1 = (bf16[128,1,128]{0,2,1:T(8,128)(2,1)S(1)}, bf16[128,1,128]{0,2,1:T(8,128)(2,1)S(1)}, u32[]{:S(2)}, u32[]{:S(2)}) collective-permute-start(bf16[128,1,128]{0,2,1:T(8,128)(2,1)S(1)} %get-tuple-element.98), channel_id=1, source_target_pairs={{0,32},{32,64},{64,96},{96,128},{128,160},{160,192},{192,224},{224... | collective-permute-start | bytes 98312 | tf_op jit(solution)/shard_map/ppermute | solution.py:16
  21.6 11.1 %collective-permute-start.2 = (bf16[128,1,128]{0,2,1:T(8,128)(2,1)S(1)}, bf16[128,1,128]{0,2,1:T(8,128)(2,1)S(1)}, u32[]{:S(2)}, u32[]{:S(2)}) collective-permute-start(bf16[128,1,128]{0,2,1:T(8,128)(2,1)S(1)} %get-tuple-element.99), channel_id=1, source_target_pairs={{32,0},{64,32},{96,64},{128,96},{160,128},{192,160},{224,192},{256... | collective-permute-start | bytes 98312 | tf_op jit(solution)/shard_map/ppermute | solution.py:18
  23.6 9.2 %collective-permute-start = (bf16[128,2,128]{0,2,1:T(8,128)(2,1)S(1)}, bf16[128,2,128]{0,2,1:T(8,128)(2,1)S(1)}, u32[]{:S(2)}, u32[]{:S(2)}) collective-permute-start(bf16[128,2,128]{0,2,1:T(8,128)(2,1)S(1)} %pad_maximum_fusion.13), channel_id=1, source_target_pairs={{0,16},{1,17},{2,18},{3,19},{4,20},{5,21},{6,22},{7,23},{8,24},{9,... | collective-permute-start | bytes 196616 | tf_op jit(solution)/shard_map/ppermute | solution.py:28
  31.4 1.3 copy-start.11
  33.2 13.2 %collective-permute-start.3 = (bf16[128,10,1]{0,2,1:T(2,128)(2,1)S(1)}, bf16[128,10,1]{0,2,1:T(2,128)(2,1)S(1)}, u32[]{:S(2)}, u32[]{:S(2)}) collective-permute-start(bf16[128,10,1]{0,2,1:T(2,128)(2,1)S(1)} %get-tuple-element.94), channel_id=1, source_target_pairs={{0,1},{1,2},{2,3},{3,4},{4,5},{5,6},{6,7},{7,8},{8,9},{9,10},{10,1... | collective-permute-start | bytes 7688 | tf_op jit(solution)/shard_map/ppermute | solution.py:16
  36.3 10.1 %collective-permute-start.4 = (bf16[128,10,1]{0,2,1:T(2,128)(2,1)S(1)}, bf16[128,10,1]{0,2,1:T(2,128)(2,1)S(1)}, u32[]{:S(2)}, u32[]{:S(2)}) collective-permute-start(bf16[128,10,1]{0,2,1:T(2,128)(2,1)S(1)} %get-tuple-element.95), channel_id=1, source_target_pairs={{1,0},{2,1},{3,2},{4,3},{5,4},{6,5},{7,6},{8,7},{9,8},{10,9},{11,1... | collective-permute-start | bytes 7688 | tf_op jit(solution)/shard_map/ppermute | solution.py:18
  46.8 4.3 copy-start.6
  46.8 5.5 %copy-start.4 = (bf16[128,10,129]{0,2,1:T(8,128)(2,1)}, bf16[128,10,129]{0,2,1:T(8,128)(2,1)S(1)}, u32[]{:S(2)}) copy-start(bf16[128,10,129]{0,2,1:T(8,128)(2,1)S(1)} %get-tuple-element.93) | copy-start | bytes 990724
  59.0 2.6 copy-start
  63.1 1.3 copy-start.3
  63.1 1.3 copy-start.15
  64.4 3.9 copy-start.9
  64.4 3.9 copy-start.14
  68.3 1.0 copy-start.12
  68.3 1.0 copy-start.13
  68.3 1.0 copy-start.10
  69.3 1.2 copy-start.8
  70.5 1.0 copy-start.7
  72.4 12.4 %copy-start.5 = (bf16[128,10,129]{0,2,1:T(8,128)(2,1)S(1)}, bf16[128,10,129]{0,2,1:T(8,128)(2,1)}, u32[]{:S(2)}) copy-start(bf16[128,10,129]{0,2,1:T(8,128)(2,1)} %copy-done.4) | copy-start | bytes 990724
  72.6 125.5 %collective-permute-start.6 = (bf16[256,1,128]{2,1,0:T(2,128)(2,1)S(1)}, bf16[256,1,128]{2,1,0:T(2,128)(2,1)S(1)}, u32[]{:S(2)}, u32[]{:S(2)}) collective-permute-start(bf16[256,1,128]{2,1,0:T(2,128)(2,1)S(1)} %get-tuple-element.96), channel_id=1, source_target_pairs={{0,32},{32,64},{64,96},{96,128},{128,160},{160,192},{192,224},{224... | collective-permute-start | bytes 196616 | tf_op jit(solution)/shard_map/ppermute | solution.py:16
  81.9 116.2 %collective-permute-start.7 = (bf16[256,1,128]{2,1,0:T(2,128)(2,1)S(1)}, bf16[256,1,128]{2,1,0:T(2,128)(2,1)S(1)}, u32[]{:S(2)}, u32[]{:S(2)}) collective-permute-start(bf16[256,1,128]{2,1,0:T(2,128)(2,1)S(1)} %get-tuple-element.97), channel_id=1, source_target_pairs={{32,0},{64,32},{96,64},{128,96},{160,128},{192,160},{224,192},{256... | collective-permute-start | bytes 196616 | tf_op jit(solution)/shard_map/ppermute | solution.py:18
  90.8 107.3 %collective-permute-start.5 = (bf16[256,2,128]{2,1,0:T(2,128)(2,1)S(1)}, bf16[256,2,128]{2,1,0:T(2,128)(2,1)S(1)}, u32[]{:S(2)}, u32[]{:S(2)}) collective-permute-start(bf16[256,2,128]{2,1,0:T(2,128)(2,1)S(1)} %pad_maximum_fusion.12), channel_id=1, source_target_pairs={{0,16},{1,17},{2,18},{3,19},{4,20},{5,21},{6,22},{7,23},{8,24},{9,... | collective-permute-start | bytes 393224 | tf_op jit(solution)/shard_map/ppermute | solution.py:28
  200.5 10.7 %collective-permute-start.8 = (bf16[256,10,1]{0,1,2:T(8,128)(2,1)S(1)}, bf16[256,10,1]{0,1,2:T(8,128)(2,1)S(1)}, u32[]{:S(2)}, u32[]{:S(2)}) collective-permute-start(bf16[256,10,1]{0,1,2:T(8,128)(2,1)S(1)} %copy.226), channel_id=1, source_target_pairs={{0,1},{1,2},{2,3},{3,4},{4,5},{5,6},{6,7},{7,8},{8,9},{9,10},{10,1... | collective-permute-start | bytes 15368 | tf_op jit(solution)/shard_map/ppermute | solution.py:16
  204.7 7.6 %collective-permute-start.9 = (bf16[256,10,1]{0,1,2:T(8,128)(2,1)S(1)}, bf16[256,10,1]{0,1,2:T(8,128)(2,1)S(1)}, u32[]{:S(2)}, u32[]{:S(2)}) collective-permute-start(bf16[256,10,1]{0,1,2:T(8,128)(2,1)S(1)} %copy.227), channel_id=1, source_target_pairs={{1,0},{2,1},{3,2},{4,3},{5,4},{6,5},{7,6},{8,7},{9,8},{10,9},{11,1... | collective-permute-start | bytes 15368 | tf_op jit(solution)/shard_map/ppermute | solution.py:18
  213.3 1.6 copy-start.2
Sparse Core Ops, SparseCore 0:
  211.3 265.8 all-reduce.1
where the time goes:
time: 487 us; the launch traced here: 486 us
  waiting for transfers between devices  253 us (52%)
  blocking collectives  98.2 us (20%)
  starting transfers between devices  58.8 us (12%)
  local copies, waits for them, and re-layouts  26.3 us (5%)
  matrix products  19.5 us (4%)
  other arithmetic  16.2 us (3%)
  between operations  14.6 us (3%)
    psum x1, waiting for transfers between devices, body(): lax.psum((local_kernel, local_bias), ('lat', 'lon'))  253 us
    psum x1, blocking collectives, body(): lax.psum((local_kernel, local_bias), ('lat', 'lon'))  98.2 us
    ppermute x4, starting transfers between devices, with_halo(): lax.ppermute(tail, axis, [(i, (i + 1) % count) for i in range(ends)])  27.3 us
    ppermute x4, starting transfers between devices, with_halo(): lax.ppermute(head, axis, [((i + 1) % count, i) for i in range(ends)])  16.8 us
    dot_general x9, local copies, waits for them, and re-layouts, body(): jnp.einsum('gc,crw->grw', kernel_weights[position], forward_windows[posit...  15.7 us
    ppermute x2, starting transfers between devices, shifted(): return lax.ppermute(value, axis, pairs)  14.6 us
  transfers between devices with their start and end apart: 11, of which 1 were waited for; matrix products, arithmetic and copies ran while one was open for 6% of the time, Pallas kernels for 0%

commit v1 on v0

--- a/solution.py
+++ b/solution.py
@@ -161,7 +161,7 @@
     grad_inputs = field_grad[:input_width].astype(jnp.bfloat16)
     grad_hidden = field_grad[input_width:].astype(jnp.bfloat16)
     scaling = 1.0 / math.sqrt(row_count * lax.axis_size("lat") * col_count * lax.axis_size("lon"))
-    summed_kernel, summed_bias = lax.psum((local_kernel, local_bias), ("lat", "lon"))
+    summed_kernel, summed_bias = lax.psum(lax.psum((local_kernel, local_bias), "lon"), "lat")
     grad_kernel = summed_kernel * scaling
     grad_bias = summed_bias * scaling
     return (hidden_next, cell_next, grad_inputs, grad_hidden, grad_cell, grad_kernel, grad_bias)

time: 487 us -> 734 us (1.51)
  waiting for transfers between devices: 253 us -> 472 us
  blocking collectives: 98.2 us -> 122 us
    psum x1 -> x2, waiting for transfers between devices: 253 us -> 472 us  [the longest x1 265 us: body(): lax.psum((local_kernel, local_bias), 'lon')]
    psum x1 -> x2, blocking collectives: 98.2 us -> 122 us  [the longest x1 64.7 us: body(): lax.psum((local_kernel, local_bias), 'lon')]
  transfers between devices with their start and end apart: 11 -> 12, of which waited for: 1 -> 2; matrix products, arithmetic and copies ran while one was open for 6% -> 4% of each run, Pallas kernels for 0% -> 0%
where the time goes in v1:
time: 734 us; the launch traced here: 733 us
  waiting for transfers between devices  472 us (64%)
  blocking collectives  122 us (17%)
  starting transfers between devices  58.9 us (8%)
  local copies, waits for them, and re-layouts  26.3 us (4%)
  matrix products  22.8 us (3%)
  other arithmetic  16.2 us (2%)
  between operations  14.6 us (2%)
    psum x1, waiting for transfers between devices, body(): lax.psum((local_kernel, local_bias), 'lon')  265 us
    psum x1, waiting for transfers between devices, body(): lax.psum(lax.psum((local_kernel, local_bias), 'lon'), 'lat')  208 us
    psum x1, blocking collectives, body(): lax.psum((local_kernel, local_bias), 'lon')  64.7 us
    psum x1, blocking collectives, body(): lax.psum(lax.psum((local_kernel, local_bias), 'lon'), 'lat')  57.2 us
    ppermute x4, starting transfers between devices, with_halo(): lax.ppermute(tail, axis, [(i, (i + 1) % count) for i in range(ends)])  26 us
    ppermute x4, starting transfers between devices, with_halo(): lax.ppermute(head, axis, [((i + 1) % count, i) for i in range(ends)])  18.2 us
    dot_general x9, local copies, waits for them, and re-layouts, body(): jnp.einsum('gc,crw->grw', kernel_weights[position], forward_windows[posit...  15.7 us
  transfers between devices with their start and end apart: 12, of which 2 were waited for; matrix products, arithmetic and copies ran while one was open for 4% of the time, Pallas kernels for 0%

profile of v1, /device:TPU:1, one launch (start us, length us, event | category | flops | bytes accessed | tf_op | source)
XLA Modules:
  0.0 733.2 jit_solution(12321015469565326538)
XLA Ops:
  7.2 1.1 copy.215
  8.4 1.1 copy.216
  9.6 12.0 %collective-permute-start.1 = (bf16[128,1,128]{0,2,1:T(8,128)(2,1)S(1)}, bf16[128,1,128]{0,2,1:T(8,128)(2,1)S(1)}, u32[]{:S(2)}, u32[]{:S(2)}) collective-permute-start(bf16[128,1,128]{0,2,1:T(8,128)(2,1)S(1)} %get-tuple-element.98), channel_id=1, source_target_pairs={{0,32},{32,64},{64,96},{96,128},{128,160},{160,192},{192,224},{224... | collective-permute-start | bytes 98312 | tf_op jit(solution)/shard_map/ppermute | solution.py:16
  21.6 1.9 collective-permute-start.2
  23.6 7.5 %collective-permute-start = (bf16[128,2,128]{0,2,1:T(8,128)(2,1)S(1)}, bf16[128,2,128]{0,2,1:T(8,128)(2,1)S(1)}, u32[]{:S(2)}, u32[]{:S(2)}) collective-permute-start(bf16[128,2,128]{0,2,1:T(8,128)(2,1)S(1)} %pad_maximum_fusion.13), channel_id=1, source_target_pairs={{0,16},{1,17},{2,18},{3,19},{4,20},{5,21},{6,22},{7,23},{8,24},{9,... | collective-permute-start | bytes 196616 | tf_op jit(solution)/shard_map/ppermute | solution.py:28
  31.0 0.3 fusion.105
  31.4 1.3 copy.221
  32.8 0.3 fusion.30
  33.2 3.1 collective-permute-start.3
  36.3 7.1 collective-permute-start.4
  43.4 0.4 fusion.36
  43.8 1.3 copy.218
  45.1 1.4 copy.224
  46.8 1.3 fusion.77
  48.4 1.3 fusion.74
  49.7 1.4 fusion.68
  51.1 1.3 fusion.65
  52.6 2.5 copy.217
  55.2 2.6 copy.219
  57.7 1.3 copy.220
  59.1 2.6 copy.222
  61.7 1.4 copy.223
  63.1 1.3 copy.225
  64.4 3.9 add_bitcast_fusion
  68.4 1.0 multiply_reduce_fusion
  69.4 0.9 fusion.157
  70.6 0.9 copy-done.7
  71.5 0.9 fusion.9
  72.6 9.0 %collective-permute-start.6 = (bf16[256,1,128]{2,1,0:T(2,128)(2,1)S(1)}, bf16[256,1,128]{2,1,0:T(2,128)(2,1)S(1)}, u32[]{:S(2)}, u32[]{:S(2)}) collective-permute-start(bf16[256,1,128]{2,1,0:T(2,128)(2,1)S(1)} %get-tuple-element.96), channel_id=1, source_target_pairs={{0,32},{32,64},{64,96},{96,128},{128,160},{160,192},{192,224},{224... | collective-permute-start | bytes 196616 | tf_op jit(solution)/shard_map/ppermute | solution.py:16
  81.9 1.9 collective-permute-start.7
  83.8 1.0 fusion.8
  84.9 1.0 fusion.7
  85.8 0.9 fusion.6
  86.8 1.0 fusion.5
  87.8 1.0 fusion.4
  88.8 0.9 fusion.3
  89.8 1.0 fusion.2
  90.8 7.1 collective-permute-start.5
  98.0 1.0 fusion.1
  98.9 1.0 fusion.18
  100.0 64.7 %psum.30 = f32[256]{0:T(256)S(1)} all-reduce(f32[256]{0:T(256)S(1)} %fusion.18), channel_id=1, replica_groups=mesh['lat'=16,'lon'=32] {'lon'}, use_global_device_ids=true, to_apply=%region_4.5 | all-reduce | flops 256 | bytes 2048 | tf_op jit(solution)/shard_map/psum | solution.py:164
  164.6 57.2 %psum.31 = f32[256]{0:T(256)S(1)} all-reduce(f32[256]{0:T(256)S(1)} %psum.30), channel_id=1, replica_groups=mesh['lat'=16,'lon'=32] {'lat'}, use_global_device_ids=true, to_apply=%region_5.6 | all-reduce | flops 256 | bytes 2048 | tf_op jit(solution)/shard_map/psum | solution.py:164
  221.9 0.4 broadcast_select_fusion.1
  222.3 0.6 pad_maximum_fusion.1
  222.9 0.5 fusion.159
  223.4 0.9 copy.226
  224.3 1.9 collective-permute-start.8
  226.2 0.9 copy.227
  227.1 7.3 collective-permute-start.9
  234.4 0.6 broadcast_multiply_fusion.1
  235.1 1.0 copy.228
  236.1 1.0 copy.229
  237.1 1.5 pad_maximum_fusion.4
  239.1 2.7 maximum_select_fusion
  241.8 1.4 fusion.158
  245.7 264.5 %all-reduce.3.cloned.1.call-done = f32[9,256,128]{2,1,0:T(8,128)} async-done(((f32[9,256,128]{2,1,0:T(8,128)}), f32[9,256,128]{2,1,0:T(8,128)}) %all-reduce.3.cloned.1.call-update) | async-done | bytes 1179664 | tf_op jit(solution)/shard_map/psum | solution.py:164
  510.2 1.1 convolution_add_fusion.11
  511.2 1.1 fusion
  512.4 1.1 fusion.15
  513.4 1.1 fusion.17
  514.6 0.7 copy.268
  515.3 0.7 copy.269
  516.1 207.9 %all-reduce.5.cloned.1.call-done = f32[9,256,128]{2,1,0:T(8,128)} async-done(((f32[9,256,128]{2,1,0:T(8,128)}), f32[9,256,128]{2,1,0:T(8,128)}) %all-reduce.5.cloned.1.call-update) | async-done | bytes 1179664 | tf_op jit(solution)/shard_map/psum | solution.py:164
  724.0 2.4 broadcast_multiply_fusion
  (72 shorter events, 5.0 us)
Async XLA Ops:
  7.2 23.9 %copy-start.1 = (bf16[9,256,128]{2,1,0:T(8,128)(2,1)S(1)}, bf16[9,256,128]{2,1,0:T(8,128)(2,1)}, u32[]{:S(2)}) copy-start(bf16[9,256,128]{2,1,0:T(8,128)(2,1)} %param.17) | copy-start | bytes 1769476
  7.2 503.0 %all-reduce.3.cloned.1.call-start = ((), (), s32[]{:S(2)}) async-start(), calls=%async_computation | async-start | bytes 2359296 | tf_op jit(solution)/shard_map/psum | solution.py:164
  9.6 23.1 %collective-permute-start.1 = (bf16[128,1,128]{0,2,1:T(8,128)(2,1)S(1)}, bf16[128,1,128]{0,2,1:T(8,128)(2,1)S(1)}, u32[]{:S(2)}, u32[]{:S(2)}) collective-permute-start(bf16[128,1,128]{0,2,1:T(8,128)(2,1)S(1)} %get-tuple-element.98), channel_id=1, source_target_pairs={{0,32},{32,64},{64,96},{96,128},{128,160},{160,192},{192,224},{224... | collective-permute-start | bytes 98312 | tf_op jit(solution)/shard_map/ppermute | solution.py:16
  21.6 11.1 %collective-permute-start.2 = (bf16[128,1,128]{0,2,1:T(8,128)(2,1)S(1)}, bf16[128,1,128]{0,2,1:T(8,128)(2,1)S(1)}, u32[]{:S(2)}, u32[]{:S(2)}) collective-permute-start(bf16[128,1,128]{0,2,1:T(8,128)(2,1)S(1)} %get-tuple-element.99), channel_id=1, source_target_pairs={{32,0},{64,32},{96,64},{128,96},{160,128},{192,160},{224,192},{256... | collective-permute-start | bytes 98312 | tf_op jit(solution)/shard_map/ppermute | solution.py:18
  23.6 9.2 %collective-permute-start = (bf16[128,2,128]{0,2,1:T(8,128)(2,1)S(1)}, bf16[128,2,128]{0,2,1:T(8,128)(2,1)S(1)}, u32[]{:S(2)}, u32[]{:S(2)}) collective-permute-start(bf16[128,2,128]{0,2,1:T(8,128)(2,1)S(1)} %pad_maximum_fusion.13), channel_id=1, source_target_pairs={{0,16},{1,17},{2,18},{3,19},{4,20},{5,21},{6,22},{7,23},{8,24},{9,... | collective-permute-start | bytes 196616 | tf_op jit(solution)/shard_map/ppermute | solution.py:28
  31.4 1.3 copy-start.11
  33.2 13.3 %collective-permute-start.3 = (bf16[128,10,1]{0,2,1:T(2,128)(2,1)S(1)}, bf16[128,10,1]{0,2,1:T(2,128)(2,1)S(1)}, u32[]{:S(2)}, u32[]{:S(2)}) collective-permute-start(bf16[128,10,1]{0,2,1:T(2,128)(2,1)S(1)} %get-tuple-element.94), channel_id=1, source_target_pairs={{0,1},{1,2},{2,3},{3,4},{4,5},{5,6},{6,7},{7,8},{8,9},{9,10},{10,1... | collective-permute-start | bytes 7688 | tf_op jit(solution)/shard_map/ppermute | solution.py:16
  36.3 10.1 %collective-permute-start.4 = (bf16[128,10,1]{0,2,1:T(2,128)(2,1)S(1)}, bf16[128,10,1]{0,2,1:T(2,128)(2,1)S(1)}, u32[]{:S(2)}, u32[]{:S(2)}) collective-permute-start(bf16[128,10,1]{0,2,1:T(2,128)(2,1)S(1)} %get-tuple-element.95), channel_id=1, source_target_pairs={{1,0},{2,1},{3,2},{4,3},{5,4},{6,5},{7,6},{8,7},{9,8},{10,9},{11,1... | collective-permute-start | bytes 7688 | tf_op jit(solution)/shard_map/ppermute | solution.py:18
  46.8 4.3 copy-start.6
  46.8 5.5 copy-start.4
  59.1 2.6 copy-start
  63.1 1.3 copy-start.3
  63.1 1.3 copy-start.15
  64.4 3.9 copy-start.9
  64.4 3.9 copy-start.14
  68.3 1.0 copy-start.12
  68.3 1.0 copy-start.13
  68.4 1.0 copy-start.10
  69.3 1.2 copy-start.8
  70.5 1.0 copy-start.7
  72.5 12.4 %copy-start.5 = (bf16[128,10,129]{0,2,1:T(8,128)(2,1)S(1)}, bf16[128,10,129]{0,2,1:T(8,128)(2,1)}, u32[]{:S(2)}) copy-start(bf16[128,10,129]{0,2,1:T(8,128)(2,1)} %copy-done.4) | copy-start | bytes 990724
  72.6 149.2 %collective-permute-start.6 = (bf16[256,1,128]{2,1,0:T(2,128)(2,1)S(1)}, bf16[256,1,128]{2,1,0:T(2,128)(2,1)S(1)}, u32[]{:S(2)}, u32[]{:S(2)}) collective-permute-start(bf16[256,1,128]{2,1,0:T(2,128)(2,1)S(1)} %get-tuple-element.96), channel_id=1, source_target_pairs={{0,32},{32,64},{64,96},{96,128},{128,160},{160,192},{192,224},{224... | collective-permute-start | bytes 196616 | tf_op jit(solution)/shard_map/ppermute | solution.py:16
  81.9 140.0 %collective-permute-start.7 = (bf16[256,1,128]{2,1,0:T(2,128)(2,1)S(1)}, bf16[256,1,128]{2,1,0:T(2,128)(2,1)S(1)}, u32[]{:S(2)}, u32[]{:S(2)}) collective-permute-start(bf16[256,1,128]{2,1,0:T(2,128)(2,1)S(1)} %get-tuple-element.97), channel_id=1, source_target_pairs={{32,0},{64,32},{96,64},{128,96},{160,128},{192,160},{224,192},{256... | collective-permute-start | bytes 196616 | tf_op jit(solution)/shard_map/ppermute | solution.py:18
  90.8 131.1 %collective-permute-start.5 = (bf16[256,2,128]{2,1,0:T(2,128)(2,1)S(1)}, bf16[256,2,128]{2,1,0:T(2,128)(2,1)S(1)}, u32[]{:S(2)}, u32[]{:S(2)}) collective-permute-start(bf16[256,2,128]{2,1,0:T(2,128)(2,1)S(1)} %pad_maximum_fusion.12), channel_id=1, source_target_pairs={{0,16},{1,17},{2,18},{3,19},{4,20},{5,21},{6,22},{7,23},{8,24},{9,... | collective-permute-start | bytes 393224 | tf_op jit(solution)/shard_map/ppermute | solution.py:28
  224.3 10.7 %collective-permute-start.8 = (bf16[256,10,1]{0,1,2:T(8,128)(2,1)S(1)}, bf16[256,10,1]{0,1,2:T(8,128)(2,1)S(1)}, u32[]{:S(2)}, u32[]{:S(2)}) collective-permute-start(bf16[256,10,1]{0,1,2:T(8,128)(2,1)S(1)} %copy.226), channel_id=1, source_target_pairs={{0,1},{1,2},{2,3},{3,4},{4,5},{5,6},{6,7},{7,8},{8,9},{9,10},{10,1... | collective-permute-start | bytes 15368 | tf_op jit(solution)/shard_map/ppermute | solution.py:16
  227.1 8.9 %collective-permute-start.9 = (bf16[256,10,1]{0,1,2:T(8,128)(2,1)S(1)}, bf16[256,10,1]{0,1,2:T(8,128)(2,1)S(1)}, u32[]{:S(2)}, u32[]{:S(2)}) collective-permute-start(bf16[256,10,1]{0,1,2:T(8,128)(2,1)S(1)} %copy.227), channel_id=1, source_target_pairs={{1,0},{2,1},{3,2},{4,3},{5,4},{6,5},{7,6},{8,7},{9,8},{10,9},{11,1... | collective-permute-start | bytes 15368 | tf_op jit(solution)/shard_map/ppermute | solution.py:18
  235.0 489.0 %all-reduce.5.cloned.1.call-start = ((), (), s32[]{:S(2)}) async-start(), calls=%async_computation.1 | async-start | bytes 2359296 | tf_op jit(solution)/shard_map/psum | solution.py:164
  237.1 1.6 copy-start.2
Sparse Core Ops, SparseCore 0:
  235.1 274.9 all-reduce.2
  513.3 210.5 all-reduce.4
